TPU v7x, 256 devices: a whole 4x4x8 slice. The times are simulated.
256 devices in a mesh: row: 32 (over x, y, z_lo), src: 8 (over z_hi, core).
Axes of the slice: x: 4, y: 4, z: 8 (z_hi: 4, z_lo: 2; z = z_hi * 2 + z_lo), core: 2. Of those that a mesh axis runs over, the one named last changes fastest.
Arguments:
- traces: bfloat16 [16384, 128, 512], P('row', 'src'), may hold values from -6 to 6
- row_source: int32 [16384], P('row'), may hold values from 0 to 16383, as said below
- slice_data: bfloat16 [2, 16384, 32, 512], P(None, 'row', None, 'src'), may hold values from -0.03125 to 0.03125
- wavelet_inverse: float32 [2], replicated, may hold values from 0.3 to 0.8
Outputs:
- multiples: float32 [16384, 2, 128], P(('row', 'src'))
- primaries: float32 [16384, 2, 128], P(('row', 'src'))
Inputs may be any that keep to these rules, and one draw needn't show every extreme that they name: `row_source`: every recording row is named exactly once; entry e * 512 + p names a recording row whose index modulo 512 lies in [e * 16, (e + 1) * 16).
All inputs are finite; a program needn't handle non-finite values.
Results may differ from a plain program's by a relative error of at most 0.0056.
Values may be sent and summed in bfloat16 or wider, within the bound.
A program may use at most 64 MiB of HBM per device.

v0:
```python
import jax
import jax.numpy as jnp
from jax import lax
from jax.sharding import PartitionSpec as P

FREQ = 61
ITERS = 3


def dft_kernel(samples):
    ticks = jnp.arange(samples, dtype=jnp.int32)
    moment = ticks.astype(jnp.float32)
    ramp_len = samples // 8
    rising = 0.5 - 0.5 * jnp.cos(jnp.pi * (moment + 0.5) / ramp_len)
    falling = 0.5 - 0.5 * jnp.cos(jnp.pi * (samples - moment - 0.5) / ramp_len)
    taper = jnp.where(
        ticks < ramp_len,
        rising,
        jnp.where(ticks >= samples - ramp_len, falling, jnp.ones_like(rising)),
    )
    wrapped = ticks * FREQ % samples
    angles = 2.0 * jnp.pi / samples * wrapped.astype(jnp.float32)
    factor = 1.0 / jnp.sqrt(jnp.float32(samples))
    table = jnp.stack([taper * jnp.cos(angles) * factor, -taper * jnp.sin(angles) * factor], axis=1)
    return table.astype(jnp.bfloat16)


def combine_parts(real_terms, imag_terms, shot_count):
    pred_real = real_terms[:, :shot_count] - imag_terms[:, shot_count:]
    pred_imag = real_terms[:, shot_count:] + imag_terms[:, :shot_count]
    return jnp.stack([pred_real, pred_imag], axis=1)


def body(traces, row_source, slice_data, wavelet_inverse):
    block_rows, shot_local, samples = traces.shape
    kernel = dft_kernel(samples)
    spectra = jnp.dot(
        traces.reshape(block_rows * shot_local, samples), kernel, preferred_element_type=jnp.float32
    )
    spectra = jnp.transpose(spectra.reshape(block_rows, shot_local, 2), (0, 2, 1)).astype(
        jnp.bfloat16
    )
    arrived = lax.all_to_all(spectra, "row", split_axis=0, concat_axis=0, tiled=True)
    group_rows = block_rows // lax.axis_size("row")
    located = row_source // block_rows * group_rows + row_source % group_rows
    ordered = arrived[located]
    slice_rows = block_rows // lax.axis_size("src")
    panel = lax.all_to_all(ordered, "src", split_axis=0, concat_axis=2, tiled=True)
    shot_count = panel.shape[2]
    base = panel.astype(jnp.float32)
    wave_real = wavelet_inverse[0]
    wave_imag = wavelet_inverse[1]
    real_data = slice_data[0].reshape(block_rows, -1)
    imag_data = slice_data[1].reshape(block_rows, -1)
    estimate = panel
    predicted = jnp.zeros((slice_rows, 2, shot_count), jnp.float32)
    primaries = base
    for iteration in range(ITERS):
        shard_rows = lax.all_gather(estimate, "row", axis=0, tiled=True)
        piece_rows = shard_rows.shape[0]
        stacked = shard_rows.reshape(piece_rows, 2 * shot_count)
        real_terms = jnp.dot(real_data, stacked, preferred_element_type=jnp.float32)
        imag_terms = jnp.dot(imag_data, stacked, preferred_element_type=jnp.float32)
        summed = lax.psum(combine_parts(real_terms, imag_terms, shot_count), "src")
        predicted = lax.dynamic_slice_in_dim(
            summed, lax.axis_index("src") * slice_rows, slice_rows, 0
        )
        next_real = base[:, 0] - (wave_real * predicted[:, 0] - wave_imag * predicted[:, 1])
        next_imag = base[:, 1] - (wave_real * predicted[:, 1] + wave_imag * predicted[:, 0])
        primaries = jnp.stack([next_real, next_imag], axis=1)
        estimate = primaries.astype(jnp.bfloat16)
    return (predicted, primaries)


def solution(mesh):
    in_specs = (P("row", "src", None), P("row"), P(None, "row", None, "src"), P())
    out_specs = (P(("row", "src"), None, None), P(("row", "src"), None, None))
    return jax.shard_map(body, mesh=mesh, in_specs=in_specs, out_specs=out_specs, check_vma=False)
```

profile of v0, /device:TPU:2, one launch (start us, length us, event | category | flops | bytes accessed | tf_op | source)
XLA Modules:
  0.0 753.8 jit_solution(3112653908474504425)
XLA Ops:
  7.3 5.6 fusion
  13.5 0.9 reshape.153
  14.3 9.0 %all-to-all-start = ((bf16[32,2,256]{2,1,0:T(2,128)(2,1)}), bf16[32,2,256]{2,1,0:T(2,128)(2,1)S(1)}, u32[]{:S(2)}, u32[]{:S(2)}) async-start(bf16[32,2,256]{2,1,0:T(2,128)(2,1)} %reshape.153), calls=%async_computation | async-start | bytes 65536 | tf_op jit(solution)/shard_map/all_to_all | solution.py:43
  23.4 7.0 all-to-all-done
  30.6 2.1 gather_fusion
  33.0 15.2 %all_to_all.23 = bf16[8,2,1024]{2,1,0:T(2,128)(2,1)S(1)} all-to-all(bf16[8,2,1024]{2,1,0:T(2,128)(2,1)S(1)} %reshape.155), channel_id=1, replica_groups=mesh['row'=32,'src'=8] {'src'}, dimensions={0} | all-to-all | bytes 65536 | tf_op jit(solution)/shard_map/all_to_all | solution.py:48
  49.4 4.0 fusion.41
  53.4 136.0 %all-gather.4.cloned.1.call-done = bf16[2048,2,128]{2,1,0:T(2,128)(2,1)} async-done(((bf16[64,2,128]{2,1,0:T(2,128)(2,1)}), bf16[2048,2,128]{2,1,0:T(2,128)(2,1)}) %all-gather.4.cloned.1.call-update) | async-done | bytes 1048592 | tf_op jit(solution)/shard_map/all_gather | solution.py:59
  189.4 2.7 convolution_bitcast_fusion.4
  192.1 0.7 convolution_bitcast_fusion.5
  193.0 0.8 pad_maximum_fusion
  194.5 80.9 %all-reduce.4.cloned.1.call-done = f32[512,2,128]{0,2,1:T(8,128)} async-done(((f32[512,2,128]{0,2,1:T(8,128)}), f32[512,2,128]{0,2,1:T(8,128)}) %all-reduce.4.cloned.1.call-update) | async-done | bytes 524304 | tf_op jit(solution)/shard_map/psum | solution.py:64
  275.5 2.1 subtract_convert_fusion.3
  278.4 144.4 %all-gather.6.cloned.1.call-done = bf16[2048,2,128]{2,1,0:T(2,128)(2,1)} async-done(((bf16[64,2,128]{2,1,0:T(2,128)(2,1)}), bf16[2048,2,128]{2,1,0:T(2,128)(2,1)}) %all-gather.6.cloned.1.call-update) | async-done | bytes 1048592 | tf_op jit(solution)/shard_map/all_gather | solution.py:59
  422.9 2.7 convolution_bitcast_fusion.2
  426.5 0.8 pad_maximum_fusion.1
  427.4 81.5 %all-reduce.6.cloned.1.call-done = f32[512,2,128]{0,2,1:T(8,128)} async-done(((f32[512,2,128]{0,2,1:T(8,128)}), f32[512,2,128]{0,2,1:T(8,128)}) %all-reduce.6.cloned.1.call-update) | async-done | bytes 524304 | tf_op jit(solution)/shard_map/psum | solution.py:64
  508.8 2.1 subtract_convert_fusion.1
  511.8 144.4 %all-gather.8.cloned.1.call-done = bf16[2048,2,128]{2,1,0:T(2,128)(2,1)} async-done(((bf16[64,2,128]{2,1,0:T(2,128)(2,1)}), bf16[2048,2,128]{2,1,0:T(2,128)(2,1)}) %all-gather.8.cloned.1.call-update) | async-done | bytes 1048592 | tf_op jit(solution)/shard_map/all_gather | solution.py:59
  656.3 2.7 convolution_bitcast_fusion
  659.8 0.8 pad_maximum_fusion.2
  660.7 81.6 %all-reduce.8.cloned.1.call-done = f32[512,2,128]{0,2,1:T(8,128)} async-done(((f32[512,2,128]{0,2,1:T(8,128)}), f32[512,2,128]{0,2,1:T(8,128)}) %all-reduce.8.cloned.1.call-update) | async-done | bytes 524304 | tf_op jit(solution)/shard_map/psum | solution.py:64
  742.3 1.0 constant_dynamic-slice_fusion
  744.0 2.1 subtract_subtract_fusion
  (46 shorter events, 7.9 us)
Async XLA Ops:
  7.3 16.1 %copy-start = (s32[512]{0:T(512)S(1)}, s32[512]{0:T(512)}, u32[]{:S(2)}) copy-start(s32[512]{0:T(512)} %param.5) | copy-start | bytes 6148
  14.3 16.1 %all-to-all-start = ((bf16[32,2,256]{2,1,0:T(2,128)(2,1)}), bf16[32,2,256]{2,1,0:T(2,128)(2,1)S(1)}, u32[]{:S(2)}, u32[]{:S(2)}) async-start(bf16[32,2,256]{2,1,0:T(2,128)(2,1)} %reshape.153), calls=%async_computation | async-start | bytes 65536 | tf_op jit(solution)/shard_map/all_to_all | solution.py:43
  23.3 166.1 %all-gather.4.cloned.1.call-start = ((), (), s32[]{:S(2)}) async-start(), calls=%async_computation.2 | async-start | bytes 1081344 | tf_op jit(solution)/shard_map/all_gather | solution.py:59
  49.4 226.1 %all-reduce.4.cloned.1.call-start = ((), (), s32[]{:S(2)}) async-start(), calls=%async_computation.3 | async-start | bytes 1048576 | tf_op jit(solution)/shard_map/psum | solution.py:64
  189.4 2.7 copy-start.2
  192.9 1.0 copy-start.1
  193.9 229.0 %all-gather.6.cloned.1.call-start = ((), (), s32[]{:S(2)}) async-start(), calls=%async_computation.4 | async-start | bytes 1081344 | tf_op jit(solution)/shard_map/all_gather | solution.py:59
  278.4 230.5 %all-reduce.6.cloned.1.call-start = ((), (), s32[]{:S(2)}) async-start(), calls=%async_computation.5 | async-start | bytes 1048576 | tf_op jit(solution)/shard_map/psum | solution.py:64
  422.9 2.7 copy-start.4
  427.3 229.0 %all-gather.8.cloned.1.call-start = ((), (), s32[]{:S(2)}) async-start(), calls=%async_computation.6 | async-start | bytes 1081344 | tf_op jit(solution)/shard_map/all_gather | solution.py:59
  511.8 230.6 %all-reduce.8.cloned.1.call-start = ((), (), s32[]{:S(2)}) async-start(), calls=%async_computation.7 | async-start | bytes 1048576 | tf_op jit(solution)/shard_map/psum | solution.py:64
  656.3 2.7 copy-start.3
Sparse Core Ops, SparseCore 0:
  49.5 139.8 all-gather.3
  194.0 81.4 all-reduce.3
  278.5 144.3 all-gather.5
  427.4 81.3 all-reduce.5
  511.9 144.3 all-gather.7
  660.8 81.4 all-reduce.7
where the time goes:
time: 754 us
  waiting for transfers between devices  676 us (90%)
  matrix products  16 us (2%)
  blocking collectives  15.2 us (2%)
  between operations  14.4 us (2%)
  local copies, waits for them, and re-layouts  13.5 us (2%)
  other arithmetic  9.38 us (1%)
  starting transfers between devices  9.22 us (1%)
    all_gather x3, waiting for transfers between devices, body(): shard_rows = lax.all_gather(estimate, 'row', axis=0, tiled=True)  425 us
    psum x3, waiting for transfers between devices, body(): summed = lax.psum(combine_parts(real_terms, imag_terms, shot_count), 'src')  244 us
    all_to_all x1, blocking collectives, body(): lax.all_to_all(ordered, 'src', split_axis=0, concat_axis=2, tiled=True)  15.2 us
  transfers between devices with their start and end apart: 7, of which 7 were waited for; matrix products, arithmetic and copies ran while one was open for 1% of the time, Pallas kernels for 0%

commit v1 on v0

--- a/solution.py
+++ b/solution.py
@@ -5,6 +5,12 @@
 
 FREQ = 61
 ITERS = 3
+extend_the_matrix = lambda local_block, row_dim: jnp.concatenate(
+    lax.all_to_all(
+        jnp.stack([local_block for _ in range(lax.psum(1, axis_name="row"))]), "row", 0, 0
+    ),
+    axis=row_dim,
+)
 
 
 def dft_kernel(samples):
@@ -56,7 +62,7 @@
     predicted = jnp.zeros((slice_rows, 2, shot_count), jnp.float32)
     primaries = base
     for iteration in range(ITERS):
-        shard_rows = lax.all_gather(estimate, "row", axis=0, tiled=True)
+        shard_rows = extend_the_matrix(estimate, row_dim=0)
         piece_rows = shard_rows.shape[0]
         stacked = shard_rows.reshape(piece_rows, 2 * shot_count)
         real_terms = jnp.dot(real_data, stacked, preferred_element_type=jnp.float32)

time: 754 us -> 356 us (0.47)
  waiting for transfers between devices: 676 us -> 232 us
  blocking collectives: 15.2 us -> 58.6 us
    all_gather x3 -> x0, waiting for transfers between devices: 425 us -> none  [body(): shard_rows = lax.all_gather(estimate, 'row', axis=0, tiled=True)]
    all_to_all x0 -> x2, blocking collectives: none -> 43.3 us  [lax.all_to_all(jnp.stack([local_block for _ in range(lax.psum(1, axis_nam...]
    psum x3, waiting for transfers between devices: 244 us -> 213 us  [body(): summed = lax.psum(combine_parts(real_terms, imag_terms, shot_count), 'src')]
    all_to_all x0 -> x1, waiting for transfers between devices: none -> 11.5 us  [lax.all_to_all(jnp.stack([local_block for _ in range(lax.psum(1, axis_nam...]
  transfers between devices with their start and end apart: 7 -> 5, of which waited for: 7 -> 5; matrix products, arithmetic and copies ran while one was open for 1% -> 1% of each run, Pallas kernels for 0% -> 0%
where the time goes in v1:
time: 356 us
  waiting for transfers between devices  232 us (65%)
  blocking collectives  58.6 us (16%)
  local copies, waits for them, and re-layouts  15.6 us (4%)
  starting transfers between devices  14.1 us (4%)
  between operations  14 us (4%)
  matrix products  11.7 us (3%)
  other arithmetic  9.91 us (3%)
    psum x3, waiting for transfers between devices, body(): summed = lax.psum(combine_parts(real_terms, imag_terms, shot_count), 'src')  213 us
    all_to_all x2, blocking collectives, lax.all_to_all(jnp.stack([local_block for _ in range(lax.psum(1, axis_nam...  43.3 us
    all_to_all x1, blocking collectives, body(): lax.all_to_all(ordered, 'src', split_axis=0, concat_axis=2, tiled=True)  15.2 us
    all_to_all x1, waiting for transfers between devices, lax.all_to_all(jnp.stack([local_block for _ in range(lax.psum(1, axis_nam...  11.5 us
    all_to_all x1, starting transfers between devices, body(): lax.all_to_all(spectra, 'row', split_axis=0, concat_axis=0, tiled=True)  8.97 us
  transfers between devices with their start and end apart: 5, of which 5 were waited for; matrix products, arithmetic and copies ran while one was open for 1% of the time, Pallas kernels for 0%

profile of v1, /device:TPU:2, one launch (start us, length us, event | category | flops | bytes accessed | tf_op | source)
XLA Modules:
  0.0 355.7 jit_solution(6910822759453488916)
XLA Ops:
  7.3 5.6 %fusion = bf16[8192,2]{0,1:T(2,128)(2,1)S(1)} fusion(bf16[8192,512]{1,0:T(8,128)(2,1)} %bitcast.69, bf16[512,1]{0,1:T(2,128)(2,1)S(1)} %get-tuple-element.24, bf16[512,1]{0,1:T(2,128)(2,1)S(1)} %get-tuple-element.25), kind=kOutput, calls=%fused_computation.2 | convolution fusion | flops 16797696 | bytes 8423424 | tf_op jit(solution)/shard_map/dot_general | solution.py:43
  13.5 0.9 reshape.158
  14.3 9.0 %all-to-all-start = ((bf16[32,2,256]{2,1,0:T(2,128)(2,1)}), bf16[32,2,256]{2,1,0:T(2,128)(2,1)S(1)}, u32[]{:S(2)}, u32[]{:S(2)}) async-start(bf16[32,2,256]{2,1,0:T(2,128)(2,1)} %reshape.158), calls=%async_computation | async-start | bytes 65536 | tf_op jit(solution)/shard_map/all_to_all | solution.py:49
  23.3 7.1 %all-to-all-done = bf16[32,2,256]{2,1,0:T(2,128)(2,1)S(1)} async-done(((bf16[32,2,256]{2,1,0:T(2,128)(2,1)}), bf16[32,2,256]{2,1,0:T(2,128)(2,1)S(1)}, u32[]{:S(2)}, u32[]{:S(2)}) %all-to-all-start) | async-done | bytes 32800 | tf_op jit(solution)/shard_map/all_to_all | solution.py:49
  30.6 2.1 gather_fusion
  33.0 15.2 %all_to_all.38 = bf16[8,2,1024]{2,1,0:T(2,128)(2,1)S(1)} all-to-all(bf16[8,2,1024]{2,1,0:T(2,128)(2,1)S(1)} %reshape.160), channel_id=1, replica_groups=mesh['row'=32,'src'=8] {'src'}, dimensions={0} | all-to-all | bytes 65536 | tf_op jit(solution)/shard_map/all_to_all | solution.py:54
  48.7 1.9 stack.34
  50.7 5.0 %all-to-all-start.2 = ((bf16[32,64,2,128]{3,2,1,0:T(2,128)(2,1)}), bf16[32,64,2,128]{3,2,1,0:T(2,128)(2,1)S(1)}, u32[]{:S(2)}, u32[]{:S(2)}) async-start(bf16[32,64,2,128]{3,2,1,0:T(2,128)(2,1)} %stack.34), calls=%async_computation.2 | async-start | bytes 2097152 | tf_op jit(solution)/shard_map/all_to_all | solution.py:9
  55.7 4.1 %fusion.41 = (bf16[1,512,32,64]{1,3,2,0:T(8,128)(2,1)S(1)}, bf16[1,512,32,64]{1,3,2,0:T(8,128)(2,1)}) fusion(bf16[2,512,32,64]{1,3,2,0:T(8,128)(2,1)} %param.6), kind=kLoop, calls=%fused_computation.88 | loop fusion | bytes 8388608 | tf_op jit(solution)/shard_map/slice | solution.py:59
  59.8 11.5 %all-to-all-done.2 = bf16[32,64,2,128]{3,2,1,0:T(2,128)(2,1)S(1)} async-done(((bf16[32,64,2,128]{3,2,1,0:T(2,128)(2,1)}), bf16[32,64,2,128]{3,2,1,0:T(2,128)(2,1)S(1)}, u32[]{:S(2)}, u32[]{:S(2)}) %all-to-all-start.2) | async-done | bytes 1048608 | tf_op jit(solution)/shard_map/all_to_all | solution.py:9
  71.3 2.3 convolution_bitcast_fusion.4
  74.4 0.8 pad_maximum_fusion
  76.1 68.6 %all-reduce.4.cloned.1.call-done = f32[512,2,128]{0,2,1:T(8,128)} async-done(((f32[512,2,128]{0,2,1:T(8,128)}), f32[512,2,128]{0,2,1:T(8,128)}) %all-reduce.4.cloned.1.call-update) | async-done | bytes 524304 | tf_op jit(solution)/shard_map/psum | solution.py:70
  144.6 2.3 subtract_convert_fusion.3
  147.1 0.9 stack.39
  148.0 21.7 %all_to_all.39 = bf16[32,64,2,128]{3,2,1,0:T(2,128)(2,1)S(1)} all-to-all(bf16[32,64,2,128]{3,2,1,0:T(2,128)(2,1)S(1)} %stack.39), channel_id=1, replica_groups=mesh['row'=32,'src'=8] {'row'}, dimensions={0} | all-to-all | bytes 2097152 | tf_op jit(solution)/shard_map/all_to_all | solution.py:9
  172.2 72.4 %all-reduce.6.cloned.1.call-done = f32[512,2,128]{0,2,1:T(8,128)} async-done(((f32[512,2,128]{0,2,1:T(8,128)}), f32[512,2,128]{0,2,1:T(8,128)}) %all-reduce.6.cloned.1.call-update) | async-done | bytes 524304 | tf_op jit(solution)/shard_map/psum | solution.py:70
  244.5 2.3 subtract_convert_fusion.1
  247.0 0.9 stack.44
  248.0 21.7 %all_to_all.40 = bf16[32,64,2,128]{3,2,1,0:T(2,128)(2,1)S(1)} all-to-all(bf16[32,64,2,128]{3,2,1,0:T(2,128)(2,1)S(1)} %stack.44), channel_id=1, replica_groups=mesh['row'=32,'src'=8] {'row'}, dimensions={0} | all-to-all | bytes 2097152 | tf_op jit(solution)/shard_map/all_to_all | solution.py:9
  271.2 0.8 pad_maximum_fusion.2
  272.1 72.3 %all-reduce.8.cloned.1.call-done = f32[512,2,128]{0,2,1:T(8,128)} async-done(((f32[512,2,128]{0,2,1:T(8,128)}), f32[512,2,128]{0,2,1:T(8,128)}) %all-reduce.8.cloned.1.call-update) | async-done | bytes 524304 | tf_op jit(solution)/shard_map/psum | solution.py:70
  344.4 1.0 constant_dynamic-slice_fusion
  346.1 2.3 subtract_subtract_fusion
  (42 shorter events, 8.9 us)
Async XLA Ops:
  7.3 16.0 %copy-start.2 = (s32[512]{0:T(512)S(1)}, s32[512]{0:T(512)}, u32[]{:S(2)}) copy-start(s32[512]{0:T(512)} %param.5) | copy-start | bytes 6148
  14.3 16.1 %all-to-all-start = ((bf16[32,2,256]{2,1,0:T(2,128)(2,1)}), bf16[32,2,256]{2,1,0:T(2,128)(2,1)S(1)}, u32[]{:S(2)}, u32[]{:S(2)}) async-start(bf16[32,2,256]{2,1,0:T(2,128)(2,1)} %reshape.158), calls=%async_computation | async-start | bytes 65536 | tf_op jit(solution)/shard_map/all_to_all | solution.py:49
  50.7 20.6 %all-to-all-start.2 = ((bf16[32,64,2,128]{3,2,1,0:T(2,128)(2,1)}), bf16[32,64,2,128]{3,2,1,0:T(2,128)(2,1)S(1)}, u32[]{:S(2)}, u32[]{:S(2)}) async-start(bf16[32,64,2,128]{3,2,1,0:T(2,128)(2,1)} %stack.34), calls=%async_computation.2 | async-start | bytes 2097152 | tf_op jit(solution)/shard_map/all_to_all | solution.py:9
  55.7 88.9 %all-reduce.4.cloned.1.call-start = ((), (), s32[]{:S(2)}) async-start(), calls=%async_computation.5 | async-start | bytes 1048576 | tf_op jit(solution)/shard_map/psum | solution.py:70
  74.3 1.0 copy-start.3
  75.3 169.2 %all-reduce.6.cloned.1.call-start = ((), (), s32[]{:S(2)}) async-start(), calls=%async_computation.6 | async-start | bytes 1048576 | tf_op jit(solution)/shard_map/psum | solution.py:70
  147.1 22.6 %copy-start = (bf16[1,512,32,64]{1,3,2,0:T(8,128)(2,1)S(1)}, bf16[1,512,32,64]{1,3,2,0:T(8,128)(2,1)}, u32[]{:S(2)}) copy-start(bf16[1,512,32,64]{1,3,2,0:T(8,128)(2,1)} %get-tuple-element.9) | copy-start | bytes 6291460
  172.1 172.2 %all-reduce.8.cloned.1.call-start = ((), (), s32[]{:S(2)}) async-start(), calls=%async_computation.7 | async-start | bytes 1048576 | tf_op jit(solution)/shard_map/psum | solution.py:70
  247.0 22.6 %copy-start.1 = (bf16[1,512,32,64]{1,3,2,0:T(8,128)(2,1)S(1)}, bf16[1,512,32,64]{1,3,2,0:T(8,128)(2,1)}, u32[]{:S(2)}) copy-start(bf16[1,512,32,64]{1,3,2,0:T(8,128)(2,1)} %get-tuple-element.9) | copy-start | bytes 6291460
Sparse Core Ops, SparseCore 0:
  75.4 69.1 all-reduce.3
  172.3 72.2 all-reduce.5
  272.2 72.1 all-reduce.7
